TPU v7x, 128 devices: a whole 4x4x4 slice. The times are simulated.
128 devices in a mesh: pipe: 4 (over y), tensor: 32 (over z, x, core).
Axes of the slice: x: 4, y: 4, z: 4, core: 2. Of those that a mesh axis runs over, the one named last changes fastest.
Arguments:
- inputs: bfloat16 [8, 128, 8192], P(None, None, 'tensor'), may hold values from -60 to 60
- cotangent: bfloat16 [8, 128, 8192], P(None, None, 'tensor'), may hold values from -13 to 13
- norm_gain: float32 [4, 8192], P('pipe', 'tensor'), may hold values from 0.25 to 1.75
- first_factor: bfloat16 [4, 64, 128, 512], P('pipe', 'tensor'), may hold values from -0.35355339 to 0.35355339
- second_factor: bfloat16 [4, 128, 256, 256], P('pipe', 'tensor'), may hold values from -0.25 to 0.25
- third_factor: bfloat16 [4, 128, 256, 256], P('pipe', 'tensor'), may hold values from -0.3125 to 0.3125
- fourth_factor: bfloat16 [4, 64, 512, 128], P('pipe', 'tensor'), may hold values from -0.22097087 to 0.22097087
Outputs:
- section_out: bfloat16 [4, 8, 128, 8192], P('pipe', None, None, 'tensor')
- section_grad: bfloat16 [4, 8, 128, 8192], P('pipe', None, None, 'tensor')
- gain_grad: float32 [4, 8192], P('pipe', 'tensor')
- first_grad: float32 [4, 64, 128, 512], P('pipe', 'tensor')
- second_grad: float32 [4, 128, 256, 256], P('pipe', 'tensor')
- third_grad: float32 [4, 128, 256, 256], P('pipe', 'tensor')
- fourth_grad: float32 [4, 64, 512, 128], P('pipe', 'tensor')
All inputs are finite; a program needn't handle non-finite values.
Results may differ from a plain program's by a relative error of at most 0.013.
Values may be sent and summed in bfloat16 or wider, within the bound.
No kernel may reach another device: no remote copies, remote signals or barrier semaphores. Data moves between devices by JAX's collectives and lax.ppermute only.
A program may use at most 128 MiB of HBM per device.

v0:
```python
import math

import jax
import jax.numpy as jnp
from jax import lax
from jax.sharding import PartitionSpec as P

EPS = 1e-05
TANH_SCALE = math.sqrt(2.0 / math.pi)
CUBIC_COEF = 0.044715


def from_behind(array, axis, by):
    size = lax.axis_size(axis)
    pairs = [(i, i + by) for i in range(size) if 0 <= i + by < size]
    return lax.ppermute(array, axis, pairs)


def gelu_pair(preact):
    tanh_val = jnp.tanh(TANH_SCALE * (preact + CUBIC_COEF * preact * preact * preact))
    gelu_value = 0.5 * preact * (1.0 + tanh_val)
    gelu_slope = 0.5 * (1.0 + tanh_val) + 0.5 * preact * (
        1.0 - tanh_val * tanh_val
    ) * TANH_SCALE * (1.0 + 3.0 * CUBIC_COEF * preact * preact)
    return (gelu_value, gelu_slope)


def row_total(values):
    return lax.psum(values, "tensor")


def to_hidden(values):
    return lax.all_to_all(values, "tensor", split_axis=3, concat_axis=1, tiled=True)


def to_features(values):
    return lax.all_to_all(values, "tensor", split_axis=1, concat_axis=3, tiled=True)


def load_at(stored, micro_slot):
    return lax.dynamic_index_in_dim(stored, micro_slot, 0, keepdims=False)


def store_at(stored, member, micro_slot, is_valid):
    former = lax.dynamic_index_in_dim(stored, micro_slot, 0, keepdims=False)
    return lax.dynamic_update_index_in_dim(
        stored, jnp.where(is_valid, member, former), micro_slot, 0
    )


def body(inputs, cotangent, norm_gain, first_factor, second_factor, third_factor, fourth_factor):
    sections = lax.axis_size("pipe")
    section_id = lax.axis_index("pipe")
    micro_count, tokens, width_dev = inputs.shape
    full_width = width_dev * lax.axis_size("tensor")
    blocks = first_factor.shape[1]
    block_size = first_factor.shape[2]
    expand = first_factor.shape[3] // block_size
    col_blocks = second_factor.shape[1]
    mix_width = second_factor.shape[2]
    all_blocks = mix_width // expand
    gain_row = norm_gain[0]
    factor_one = first_factor[0].reshape(blocks, block_size, expand, block_size)
    factor_two = second_factor[0].reshape(col_blocks, all_blocks, expand, mix_width)
    factor_three = third_factor[0].reshape(col_blocks, mix_width, all_blocks, expand)
    factor_four = fourth_factor[0].reshape(blocks, expand, block_size, block_size)
    ticks = micro_count + sections - 1
    carry = jnp.zeros((tokens, width_dev), jnp.bfloat16)
    out_buffer = jnp.zeros((micro_count, tokens, width_dev), jnp.bfloat16)
    records = None
    for tick_now in range(ticks):
        micro_id = tick_now - section_id
        is_valid = (micro_id >= 0) & (micro_id < micro_count)
        micro_slot = jnp.clip(micro_id, 0, micro_count - 1)
        stream_in = jnp.where(section_id == 0, load_at(inputs, micro_slot), carry)
        forward_stream = stream_in.astype(jnp.float32)
        sum_sq = row_total(jnp.sum(forward_stream * forward_stream, axis=-1))
        forward_inv_rms = lax.rsqrt(sum_sq / full_width + EPS)
        forward_normed = (forward_stream * forward_inv_rms[:, None] * gain_row).astype(jnp.bfloat16)
        spread = jnp.einsum(
            "tij,ijak->tiak",
            forward_normed.reshape(tokens, blocks, block_size),
            factor_one,
            preferred_element_type=jnp.float32,
        ).astype(jnp.bfloat16)
        forward_hidden_in = to_hidden(spread)
        activations_preact = jnp.einsum(
            "tiac,ciae->tce", forward_hidden_in, factor_two, preferred_element_type=jnp.float32
        )
        activations_gelu_value, activations_gelu_slope = gelu_pair(activations_preact)
        middle_activated = activations_gelu_value.astype(jnp.bfloat16)
        mixed_out = jnp.einsum(
            "tce,ceia->tiac", middle_activated, factor_three, preferred_element_type=jnp.float32
        ).astype(jnp.bfloat16)
        forward_feature_in = to_features(mixed_out)
        branch = jnp.einsum(
            "tiak,iakj->tij", forward_feature_in, factor_four, preferred_element_type=jnp.float32
        )
        forward_branch = branch.reshape(forward_feature_in.shape[0], width_dev)
        result = (forward_stream + forward_branch).astype(jnp.bfloat16)
        forward_record = (
            stream_in,
            forward_inv_rms,
            forward_hidden_in,
            forward_feature_in,
            activations_preact,
            middle_activated,
        )
        result, record = (result, forward_record)
        out_buffer = store_at(out_buffer, result, micro_slot, is_valid)
        if records is None:
            records = [jnp.zeros((micro_count,) + member.shape, member.dtype) for member in record]
        records = [
            store_at(stored, member, micro_slot, is_valid)
            for stored, member in zip(records, record)
        ]
        if tick_now + 1 < ticks:
            carry = from_behind(result, "pipe", 1)
    grad_carry = jnp.zeros((tokens, width_dev), jnp.bfloat16)
    grad_buffer = jnp.zeros((micro_count, tokens, width_dev), jnp.bfloat16)
    running = [
        jnp.zeros((width_dev,), jnp.float32),
        jnp.zeros((blocks, block_size, expand, block_size), jnp.float32),
        jnp.zeros((col_blocks, all_blocks, expand, mix_width), jnp.float32),
        jnp.zeros((col_blocks, mix_width, all_blocks, expand), jnp.float32),
        jnp.zeros((blocks, expand, block_size, block_size), jnp.float32),
    ]
    for tick_now in range(ticks):
        micro_id = tick_now - (sections - 1 - section_id)
        is_valid = (micro_id >= 0) & (micro_id < micro_count)
        micro_slot = jnp.clip(micro_id, 0, micro_count - 1)
        grad_out = jnp.where(section_id == sections - 1, load_at(cotangent, micro_slot), grad_carry)
        record = tuple((load_at(stored, micro_slot) for stored in records))
        backward_stream_in, inv_rms, hidden_in, feature_in, preact, activated = record
        stream = backward_stream_in.astype(jnp.float32)
        inv_col = inv_rms[:, None]
        grad_blocks = grad_out.reshape(tokens, blocks, block_size)
        backward_part_four = jnp.einsum(
            "tiak,tij->iakj", feature_in, grad_blocks, preferred_element_type=jnp.float32
        )
        grad_feat = jnp.einsum(
            "tij,iakj->tiak", grad_blocks, factor_four, preferred_element_type=jnp.float32
        ).astype(jnp.bfloat16)
        grad_hidden = to_hidden(grad_feat)
        backward_part_three = jnp.einsum(
            "tce,tiac->ceia", activated, grad_hidden, preferred_element_type=jnp.float32
        )
        grad_act = jnp.einsum(
            "tiac,ceia->tce", grad_hidden, factor_three, preferred_element_type=jnp.float32
        )
        gelu_value, gelu_slope = gelu_pair(preact)
        grad_pre = (grad_act * gelu_slope).astype(jnp.bfloat16)
        backward_part_two = jnp.einsum(
            "tiac,tce->ciae", hidden_in, grad_pre, preferred_element_type=jnp.float32
        )
        grad_mix = jnp.einsum(
            "tce,ciae->tiac", grad_pre, factor_two, preferred_element_type=jnp.float32
        ).astype(jnp.bfloat16)
        grad_spread = to_features(grad_mix)
        normed = (
            (stream * inv_col * gain_row).astype(jnp.bfloat16).reshape(tokens, blocks, block_size)
        )
        backward_part_one = jnp.einsum(
            "tij,tiak->ijak", normed, grad_spread, preferred_element_type=jnp.float32
        )
        grad_norm = jnp.einsum(
            "tiak,ijak->tij", grad_spread, factor_one, preferred_element_type=jnp.float32
        ).reshape(tokens, width_dev)
        backward_part_gain = jnp.sum(grad_norm * stream * inv_col, axis=0)
        scaled_grad = grad_norm * gain_row
        inner_sum = row_total(jnp.sum(scaled_grad * stream, axis=-1))[:, None]
        grad_in = (
            grad_out.astype(jnp.float32)
            + scaled_grad * inv_col
            - stream * inv_col * inv_col * inv_col * inner_sum / full_width
        ).astype(jnp.bfloat16)
        grad_in, parts = (
            grad_in,
            (
                backward_part_gain,
                backward_part_one,
                backward_part_two,
                backward_part_three,
                backward_part_four,
            ),
        )
        running = [
            total + jnp.where(is_valid, member, 0.0) for total, member in zip(running, parts)
        ]
        grad_buffer = store_at(grad_buffer, grad_in, micro_slot, is_valid)
        if tick_now + 1 < ticks:
            grad_carry = from_behind(grad_in, "pipe", -1)
    part_gain, part_one, part_two, part_three, part_four = running
    return (
        out_buffer[None],
        grad_buffer[None],
        part_gain[None],
        part_one.reshape(1, blocks, block_size, expand * block_size),
        part_two.reshape(1, col_blocks, mix_width, mix_width),
        part_three.reshape(1, col_blocks, mix_width, mix_width),
        part_four.reshape(1, blocks, expand * block_size, block_size),
    )


def solution(mesh):
    placed = (
        P(None, None, "tensor"),
        P(None, None, "tensor"),
        P("pipe", "tensor"),
        P("pipe", "tensor", None, None),
        P("pipe", "tensor", None, None),
        P("pipe", "tensor", None, None),
        P("pipe", "tensor", None, None),
    )
    return jax.shard_map(
        body,
        mesh=mesh,
        in_specs=placed,
        out_specs=(
            P("pipe", None, None, "tensor"),
            P("pipe", None, None, "tensor"),
            P("pipe", "tensor"),
            P("pipe", "tensor", None, None),
            P("pipe", "tensor", None, None),
            P("pipe", "tensor", None, None),
            P("pipe", "tensor", None, None),
        ),
        check_vma=False,
    )
```

profile of v0, /device:TPU:24, one launch (start us, length us, event | category | flops | bytes accessed | tf_op | source)
XLA Modules:
  0.0 2443.7 jit_solution(7076076025298770680)
XLA Ops:
  3.2 68.3 %psum.154 = f32[128]{0:T(128)S(1)} all-reduce(f32[128]{0:T(128)S(1)} %fusion.491), channel_id=1, replica_groups=mesh['pipe'=4,'tensor'=32] {'tensor'}, use_global_device_ids=true, to_apply=%region_1.2 | all-reduce | flops 128 | bytes 1024 | tf_op jit(solution)/shard_map/psum | solution.py:29
  95.8 7.4 all-to-all-start.22
  132.4 64.3 %psum.155 = f32[128]{0:T(128)S(1)} all-reduce(f32[128]{0:T(128)S(1)} %fusion.321), channel_id=1, replica_groups=mesh['pipe'=4,'tensor'=32] {'tensor'}, use_global_device_ids=true, to_apply=%region_3.4 | all-reduce | flops 128 | bytes 1024 | tf_op jit(solution)/shard_map/psum | solution.py:29
  204.9 6.5 all-to-all-done.2
  242.2 63.8 %psum.156 = f32[128]{0:T(128)S(1)} all-reduce(f32[128]{0:T(128)S(1)} %fusion.325), channel_id=1, replica_groups=mesh['pipe'=4,'tensor'=32] {'tensor'}, use_global_device_ids=true, to_apply=%region_5.6 | all-reduce | flops 128 | bytes 1024 | tf_op jit(solution)/shard_map/psum | solution.py:29
  352.9 63.9 %psum.157 = f32[128]{0:T(128)S(1)} all-reduce(f32[128]{0:T(128)S(1)} %fusion.329), channel_id=1, replica_groups=mesh['pipe'=4,'tensor'=32] {'tensor'}, use_global_device_ids=true, to_apply=%region_7.8 | all-reduce | flops 128 | bytes 1024 | tf_op jit(solution)/shard_map/psum | solution.py:29
  463.6 63.9 %psum.158 = f32[128]{0:T(128)S(1)} all-reduce(f32[128]{0:T(128)S(1)} %fusion.333), channel_id=1, replica_groups=mesh['pipe'=4,'tensor'=32] {'tensor'}, use_global_device_ids=true, to_apply=%region_9.10 | all-reduce | flops 128 | bytes 1024 | tf_op jit(solution)/shard_map/psum | solution.py:29
  574.7 63.9 %psum.159 = f32[128]{0:T(128)S(1)} all-reduce(f32[128]{0:T(128)S(1)} %fusion.337), channel_id=1, replica_groups=mesh['pipe'=4,'tensor'=32] {'tensor'}, use_global_device_ids=true, to_apply=%region_11.12 | all-reduce | flops 128 | bytes 1024 | tf_op jit(solution)/shard_map/psum | solution.py:29
  685.4 63.9 %psum.160 = f32[128]{0:T(128)S(1)} all-reduce(f32[128]{0:T(128)S(1)} %fusion.341), channel_id=1, replica_groups=mesh['pipe'=4,'tensor'=32] {'tensor'}, use_global_device_ids=true, to_apply=%region_13.14 | all-reduce | flops 128 | bytes 1024 | tf_op jit(solution)/shard_map/psum | solution.py:29
  796.1 63.9 %psum.161 = f32[128]{0:T(128)S(1)} all-reduce(f32[128]{0:T(128)S(1)} %fusion.345), channel_id=1, replica_groups=mesh['pipe'=4,'tensor'=32] {'tensor'}, use_global_device_ids=true, to_apply=%region_15.16 | all-reduce | flops 128 | bytes 1024 | tf_op jit(solution)/shard_map/psum | solution.py:29
  907.0 63.9 %psum.162 = f32[128]{0:T(128)S(1)} all-reduce(f32[128]{0:T(128)S(1)} %fusion.349), channel_id=1, replica_groups=mesh['pipe'=4,'tensor'=32] {'tensor'}, use_global_device_ids=true, to_apply=%region_17.18 | all-reduce | flops 128 | bytes 1024 | tf_op jit(solution)/shard_map/psum | solution.py:29
  1017.7 63.9 %psum.163 = f32[128]{0:T(128)S(1)} all-reduce(f32[128]{0:T(128)S(1)} %fusion.353), channel_id=1, replica_groups=mesh['pipe'=4,'tensor'=32] {'tensor'}, use_global_device_ids=true, to_apply=%region_19.20 | all-reduce | flops 128 | bytes 1024 | tf_op jit(solution)/shard_map/psum | solution.py:29
  1128.4 63.9 %psum.164 = f32[128]{0:T(128)S(1)} all-reduce(f32[128]{0:T(128)S(1)} %fusion.357), channel_id=1, replica_groups=mesh['pipe'=4,'tensor'=32] {'tensor'}, use_global_device_ids=true, to_apply=%region_21.22 | all-reduce | flops 128 | bytes 1024 | tf_op jit(solution)/shard_map/psum | solution.py:29
  1229.5 7.5 all-to-all-start.23
  1249.9 64.6 %psum.165 = f32[128]{0:T(128)S(1)} all-reduce(f32[128]{0:T(128)} %get-tuple-element.29), channel_id=1, replica_groups=mesh['pipe'=4,'tensor'=32] {'tensor'}, use_global_device_ids=true, to_apply=%region_23.24 | all-reduce | flops 128 | bytes 1024 | tf_op jit(solution)/shard_map/psum | solution.py:29
  1362.6 65.1 %psum.166 = f32[128]{0:T(128)} all-reduce(f32[128]{0:T(128)} %get-tuple-element.31), channel_id=1, replica_groups=mesh['pipe'=4,'tensor'=32] {'tensor'}, use_global_device_ids=true, to_apply=%region_25.26 | all-reduce | flops 128 | bytes 1024 | tf_op jit(solution)/shard_map/psum | solution.py:29
  1444.6 6.2 all-to-all-done.26
  1472.8 65.1 %psum.167 = f32[128]{0:T(128)} all-reduce(f32[128]{0:T(128)} %get-tuple-element.33), channel_id=1, replica_groups=mesh['pipe'=4,'tensor'=32] {'tensor'}, use_global_device_ids=true, to_apply=%region_27.28 | all-reduce | flops 128 | bytes 1024 | tf_op jit(solution)/shard_map/psum | solution.py:29
  1556.5 6.3 all-to-all-done.28
  1584.4 65.1 %psum.168 = f32[128]{0:T(128)} all-reduce(f32[128]{0:T(128)} %get-tuple-element.35), channel_id=1, replica_groups=mesh['pipe'=4,'tensor'=32] {'tensor'}, use_global_device_ids=true, to_apply=%region_29.30 | all-reduce | flops 128 | bytes 1024 | tf_op jit(solution)/shard_map/psum | solution.py:29
  1696.1 65.1 %psum.169 = f32[128]{0:T(128)} all-reduce(f32[128]{0:T(128)} %get-tuple-element.37), channel_id=1, replica_groups=mesh['pipe'=4,'tensor'=32] {'tensor'}, use_global_device_ids=true, to_apply=%region_31.32 | all-reduce | flops 128 | bytes 1024 | tf_op jit(solution)/shard_map/psum | solution.py:29
  1779.8 6.2 all-to-all-done.32
  1807.9 65.1 %psum.170 = f32[128]{0:T(128)} all-reduce(f32[128]{0:T(128)} %get-tuple-element.39), channel_id=1, replica_groups=mesh['pipe'=4,'tensor'=32] {'tensor'}, use_global_device_ids=true, to_apply=%region_33.34 | all-reduce | flops 128 | bytes 1024 | tf_op jit(solution)/shard_map/psum | solution.py:29
  1891.6 6.3 all-to-all-done.34
  1919.5 65.1 %psum.171 = f32[128]{0:T(128)} all-reduce(f32[128]{0:T(128)} %get-tuple-element.41), channel_id=1, replica_groups=mesh['pipe'=4,'tensor'=32] {'tensor'}, use_global_device_ids=true, to_apply=%region_35.36 | all-reduce | flops 128 | bytes 1024 | tf_op jit(solution)/shard_map/psum | solution.py:29
  2003.2 6.3 all-to-all-done.36
  2031.1 65.1 %psum.172 = f32[128]{0:T(128)} all-reduce(f32[128]{0:T(128)} %get-tuple-element.43), channel_id=1, replica_groups=mesh['pipe'=4,'tensor'=32] {'tensor'}, use_global_device_ids=true, to_apply=%region_37.38 | all-reduce | flops 128 | bytes 1024 | tf_op jit(solution)/shard_map/psum | solution.py:29
  2114.8 6.3 all-to-all-done.38
  2142.9 65.1 %psum.173 = f32[128]{0:T(128)} all-reduce(f32[128]{0:T(128)} %get-tuple-element.45), channel_id=1, replica_groups=mesh['pipe'=4,'tensor'=32] {'tensor'}, use_global_device_ids=true, to_apply=%region_39.40 | all-reduce | flops 128 | bytes 1024 | tf_op jit(solution)/shard_map/psum | solution.py:29
  2226.0 6.9 all-to-all-done.40
  2254.5 65.1 %psum.174 = f32[128]{0:T(128)} all-reduce(f32[128]{0:T(128)} %get-tuple-element.47), channel_id=1, replica_groups=mesh['pipe'=4,'tensor'=32] {'tensor'}, use_global_device_ids=true, to_apply=%region_41.42 | all-reduce | flops 128 | bytes 1024 | tf_op jit(solution)/shard_map/psum | solution.py:29
  2368.3 64.6 %psum.175 = f32[128]{0:T(128)S(1)} all-reduce(f32[128]{0:T(128)S(1)} %get-tuple-element.49), channel_id=1, replica_groups=mesh['pipe'=4,'tensor'=32] {'tensor'}, use_global_device_ids=true, to_apply=%region_43.44 | all-reduce | flops 128 | bytes 1024 | tf_op jit(solution)/shard_map/psum | solution.py:29
  (875 shorter events, 951.6 us)
Async XLA Ops:
  74.3 21.6 all-to-all-start
  95.8 16.2 all-to-all-start.22
  198.0 13.4 all-to-all-start.2
  218.0 13.6 all-to-all-start.3
  309.0 13.4 all-to-all-start.4
  550.3 13.8 all-to-all-start.9
  641.5 13.3 all-to-all-start.10
  882.8 13.5 all-to-all-start.15
  1084.5 13.4 all-to-all-start.18
  1104.4 13.4 all-to-all-start.19
  1195.2 13.4 all-to-all-start.20
  1215.1 14.4 all-to-all-start.21
  1229.5 16.3 all-to-all-start.23
  1327.6 13.4 all-to-all-start.24
  1437.5 13.4 all-to-all-start.26
  1455.9 13.8 all-to-all-start.27
  1549.4 13.4 all-to-all-start.28
  1567.8 13.4 all-to-all-start.29
  1661.1 13.4 all-to-all-start.30
  1679.5 13.4 all-to-all-start.31
  1772.7 13.4 all-to-all-start.32
  1791.1 13.5 all-to-all-start.33
  1884.5 13.4 all-to-all-start.34
  1902.9 13.4 all-to-all-start.35
  1996.1 13.4 all-to-all-start.36
  2014.5 13.4 all-to-all-start.37
  2107.7 13.4 all-to-all-start.38
  2126.1 13.6 all-to-all-start.39
  2219.5 13.4 all-to-all-start.40
  2237.9 13.4 all-to-all-start.41
  2332.2 13.4 all-to-all-start.42
  2352.1 13.4 all-to-all-start.43
  (174 other events, 1686.0 us)
where the time goes:
time: 2460 us; the launch traced here: 2440 us
  blocking collectives  1420 us (58%)
  starting transfers between devices  258 us (10%)
  local copies, waits for them, and re-layouts  256 us (10%)
  waiting for transfers between devices  235 us (10%)
  matrix products  175 us (7%)
  other arithmetic  93.8 us (4%)
    psum x22, blocking collectives, row_total(): return lax.psum(values, 'tensor')  1420 us
    all_to_all x22, waiting for transfers between devices, to_hidden(): lax.all_to_all(values, 'tensor', split_axis=3, concat_axis=1, tiled=True)  119 us
    all_to_all x22, starting transfers between devices, to_features(): lax.all_to_all(values, 'tensor', split_axis=1, concat_axis=3, tiled=True)  105 us
    all_to_all x22, starting transfers between devices, to_hidden(): lax.all_to_all(values, 'tensor', split_axis=3, concat_axis=1, tiled=True)  103 us
    all_to_all x22, waiting for transfers between devices, to_features(): lax.all_to_all(values, 'tensor', split_axis=1, concat_axis=3, tiled=True)  82.4 us
    dynamic_update_slice x63, other arithmetic, store_at(): lax.dynamic_update_index_in_dim(stored, jnp.where(is_valid, member, forme...  76.8 us
    dynamic_slice x47, local copies, waits for them, and re-layouts, store_at(): former = lax.dynamic_index_in_dim(stored, micro_slot, 0, keepdims=False)  73.1 us
    ppermute x20, starting transfers between devices, from_behind(): return lax.ppermute(array, axis, pairs)  50.4 us
  transfers between devices with their start and end apart: 64, of which 52 were waited for; matrix products, arithmetic and copies ran while one was open for 10% of the time, Pallas kernels for 0%

commit v1 on v0

v1 whole, which is shorter than its diff:
```python
import functools
import math

import jax
import jax.numpy as jnp
from jax import lax
from jax.experimental import pallas as pl
from jax.experimental.pallas import tpu as pltpu
from jax.sharding import PartitionSpec as P

EPS = 1e-05
TANH_SCALE = math.sqrt(2.0 / math.pi)
CUBIC_COEF = 0.044715
F32, BF16 = jnp.float32, jnp.bfloat16

ROWS_MID, ROWS_OUT = 2048, 512


def dot(lhs, rhs, contract):
    return lax.dot_general(lhs, rhs, ((contract[:1], contract[1:]), ((), ())), preferred_element_type=F32)


def nn(lhs, rhs):
    return dot(lhs, rhs, (1, 0))


def tn(lhs, rhs):
    return dot(lhs, rhs, (0, 0))


def nt(lhs, rhs):
    return dot(lhs, rhs, (1, 1))


def one_hot(hit):
    return jnp.where(hit, 1.0, 0.0).astype(BF16)


def iotas():
    return lax.broadcasted_iota(jnp.int32, (256, 256), 0), lax.broadcasted_iota(jnp.int32, (256, 256), 1)


def feature_pack():
    out, inn = iotas()
    return one_hot(inn == (out & 3) * 64 + (out >> 2))


def feature_unpack():
    out, inn = iotas()
    return one_hot(out == (inn & 3) * 64 + (inn >> 2))


def hidden_unpack():
    out, inn = iotas()
    return one_hot(inn == ((out & 63) >> 2) * 16 + (out >> 6) * 4 + (out & 3))


def hidden_pack():
    out, inn = iotas()
    return one_hot(out == ((inn & 63) >> 2) * 16 + (inn >> 6) * 4 + (inn & 3))


def lanes(parts):
    return jnp.concatenate(parts, axis=1)


def rows(parts):
    return jnp.concatenate(parts, axis=0)


def send_features(out_ref, base, values):
    pack = feature_pack()
    for i in range(2):
        part = values[i].astype(BF16)
        for group in range(2):
            picked = rows([part[a * 128 + group * 64 : a * 128 + group * 64 + 64] for a in range(4)])
            packed = nn(pack, picked).astype(BF16)
            for half in range(2):
                start = base + half * 32 + i * 16
                out_ref[group * 16 : group * 16 + 16, start : start + 16, :] = packed[
                    :, half * 128 : half * 128 + 128
                ].reshape(16, 16, 128)


def take_features(in_ref, base):
    unpack = feature_unpack()
    blocks = []
    for i in range(2):
        groups = []
        for group in range(2):
            halves = []
            for half in range(2):
                start = base + half * 32 + i * 16
                halves.append(in_ref[group * 16 : group * 16 + 16, start : start + 16, :].reshape(256, 128))
            groups.append(nn(unpack, lanes(halves)).astype(BF16))
        blocks.append(rows([groups[g][a * 64 : a * 64 + 64] for a in range(4) for g in range(2)]))
    return blocks


def send_hidden(out_ref, base, values):
    pack = hidden_pack()
    for group in range(4):
        picked = rows([values[c][group * 64 : group * 64 + 64] for c in range(4)])
        packed = nn(pack, picked).astype(BF16)
        for half in range(2):
            start = base + half * 32
            out_ref[group * 8 : group * 8 + 8, start : start + 32, :] = packed[
                :, half * 128 : half * 128 + 128
            ].reshape(8, 32, 128)


def take_hidden(in_ref, base):
    unpack = hidden_unpack()
    groups = []
    for group in range(4):
        halves = []
        for half in range(2):
            start = base + half * 32
            halves.append(in_ref[group * 8 : group * 8 + 8, start : start + 32, :].reshape(256, 128))
        groups.append(nn(unpack, lanes(halves)).astype(BF16))
    return [rows([groups[g][c * 64 : c * 64 + 64] for g in range(4)]) for c in range(4)]


def send_total(out_ref, base, total):
    high = total.astype(BF16).astype(F32)
    low = total - high
    block = rows(
        [high[:, :128], high[:, 128:], low[:, :128], low[:, 128:], jnp.zeros((4, 128), F32)]
    ).astype(BF16)
    out_ref[:, base : base + 8, :] = jnp.broadcast_to(block[None], (32, 8, 128))


def take_total(in_ref, base):
    summed = jnp.sum(in_ref[:, base : base + 8, :].astype(F32), axis=0)
    return lanes([summed[0:1] + summed[2:3], summed[1:2] + summed[3:4]])


def gelu_pair(preact):
    tanh_val = jnp.tanh(TANH_SCALE * (preact + CUBIC_COEF * preact * preact * preact))
    gelu_value = 0.5 * preact * (1.0 + tanh_val)
    gelu_slope = 0.5 * (1.0 + tanh_val) + 0.5 * preact * (
        1.0 - tanh_val * tanh_val
    ) * TANH_SCALE * (1.0 + 3.0 * CUBIC_COEF * preact * preact)
    return (gelu_value, gelu_slope)


def gain_column(gain_ref):
    row = gain_ref[0, 0:1, :].astype(F32) + gain_ref[0, 1:2, :].astype(F32) + gain_ref[0, 2:3, :].astype(F32)
    cols = []
    for i in range(2):
        square = jnp.broadcast_to(row[:, i * 128 : i * 128 + 128], (128, 128)).T
        cols.append(lanes([square, square]))
    return rows(cols)


def first_of(first_ref, i):
    return lanes([first_ref[0, h * 256 + i * 128 : h * 256 + i * 128 + 128, :] for h in range(2)])


def fourth_of(fourth_ref, i):
    return fourth_ref[0, :, i * 128 : i * 128 + 128]


def enter_layer(stream, gain_ref, first_ref, wire_ref):
    send_total(wire_ref, 64, jnp.sum(stream * stream, axis=0, keepdims=True))
    scaled = (stream * gain_column(gain_ref)).astype(BF16)
    send_features(
        wire_ref, 0, [tn(first_of(first_ref, i), scaled[i * 128 : i * 128 + 128]) for i in range(2)]
    )


def leave_layer(stream, mixed, fourth_ref):
    branch = rows([tn(fourth_of(fourth_ref, i), mixed[i]) for i in range(2)])
    return (stream + branch).astype(BF16)


def pack_kernel(first_ref, second_ref, third_ref, fourth_ref, gain_ref, out_ref):
    for copy in range(4):
        for c in range(4):
            out_ref[copy, c * 256 : c * 256 + 256, :] = second_ref[0, c]
            out_ref[copy, 1024 + c * 256 : 1024 + c * 256 + 256, :] = third_ref[0, c]
        for i in range(2):
            for h in range(2):
                start = ROWS_MID + h * 256 + i * 128
                out_ref[copy, start : start + 128, :] = first_ref[0, i, :, h * 256 : h * 256 + 256]
        start = ROWS_MID + ROWS_OUT
        out_ref[copy, start : start + ROWS_OUT, :] = lanes([fourth_ref[0, 0], fourth_ref[0, 1]])
        gain = gain_ref[...]
        high = gain.astype(BF16).astype(F32)
        mid = (gain - high).astype(BF16).astype(F32)
        low = gain - high - mid
        out_ref[copy, start + ROWS_OUT : start + ROWS_OUT + 16, :] = rows(
            [high, mid, low, jnp.zeros((13, 256), F32)]
        ).astype(BF16)


def start_kernel(slot_ref, input_ref, first_ref, gain_ref, wire_ref, stream_ref):
    stream = input_ref[...].astype(F32).reshape(256, 256).T
    stream_ref[...] = stream.astype(BF16)
    enter_layer(stream, gain_ref, first_ref, wire_ref)


def inv_rms_of(wire_ref):
    return lax.rsqrt(take_total(wire_ref, 64) / 8192.0 + EPS)


def hidden_forward_kernel(wire_ref, middle_ref, out_ref, spread_ref, preact_ref, act_ref, inv_ref):
    inv_rms = inv_rms_of(wire_ref)
    inv_ref[...] = jnp.broadcast_to(inv_rms, (8, 256))
    spread = take_hidden(wire_ref, 0)
    mixed = []
    for c in range(4):
        spread_ref[c] = spread[c]
        preact = tn(middle_ref[0, c * 256 : c * 256 + 256, :], spread[c]) * inv_rms
        preact_ref[c] = preact
        tanh_val = jnp.tanh(TANH_SCALE * (preact + CUBIC_COEF * preact * preact * preact))
        act = (0.5 * preact * (1.0 + tanh_val)).astype(BF16)
        act_ref[c] = act
        mixed.append(tn(middle_ref[0, 1024 + c * 256 : 1024 + c * 256 + 256, :], act).astype(BF16))
    send_hidden(out_ref, 0, mixed)


def between_kernel(wire_ref, stream_ref, fourth_ref, first_ref, gain_ref, out_ref, next_ref, mixed_ref, section_ref):
    mixed = take_features(wire_ref, 0)
    mixed_ref[0], mixed_ref[1] = mixed[0], mixed[1]
    result = leave_layer(stream_ref[...].astype(F32), mixed, fourth_ref)
    next_ref[...] = result
    stream = result.astype(F32)
    enter_layer(stream, gain_ref, first_ref, out_ref)
    section_ref[...] = stream.T.astype(BF16)


def turn_kernel(
    slot_ref, wire_ref, stream_ref, fourth_ref, first_ref, gain_ref, cotangent_ref, last_fourth_ref,
    out_ref, next_ref, mixed_ref, section_ref, grad_ref,
):
    between_kernel(
        wire_ref, stream_ref, fourth_ref, first_ref, gain_ref, out_ref, next_ref, mixed_ref, section_ref
    )
    grad = cotangent_ref[...].astype(F32).reshape(256, 256).T.astype(BF16)
    grad_ref[...] = grad
    send_grad(out_ref, 72, grad, last_fourth_ref)


def send_grad(out_ref, base, grad, fourth_ref):
    send_features(
        out_ref, base, [nn(fourth_of(fourth_ref, i), grad[i * 128 : i * 128 + 128]) for i in range(2)]
    )


def hidden_backward(c, grad_mixed, act, preact, slope, inv_rms, spread, middle_ref, grads_ref):
    grads_ref[1024 + c * 256 : 1024 + c * 256 + 256, :] = nt(act, grad_mixed).astype(BF16)
    grad_act = nn(middle_ref[0, 1024 + c * 256 : 1024 + c * 256 + 256, :], grad_mixed)
    grad_pre = grad_act * slope * inv_rms
    part = jnp.sum(grad_pre * preact, axis=0, keepdims=True)
    grad_pre = grad_pre.astype(BF16)
    grads_ref[c * 256 : c * 256 + 256, :] = nt(spread, grad_pre).astype(BF16)
    return nn(middle_ref[0, c * 256 : c * 256 + 256, :], grad_pre).astype(BF16), part


def hidden_turn_kernel(wire_ref, middle_ref, out_ref, grads_ref):
    inv_rms = inv_rms_of(wire_ref)
    spread = take_hidden(wire_ref, 0)
    grad_mixed = take_hidden(wire_ref, 72)
    mixed, grad_spread, total = [], [], 0.0
    for c in range(4):
        preact = tn(middle_ref[0, c * 256 : c * 256 + 256, :], spread[c]) * inv_rms
        value, slope = gelu_pair(preact)
        act = value.astype(BF16)
        mixed.append(tn(middle_ref[0, 1024 + c * 256 : 1024 + c * 256 + 256, :], act).astype(BF16))
        grad, part = hidden_backward(
            c, grad_mixed[c], act, preact, slope, inv_rms, spread[c], middle_ref, grads_ref
        )
        grad_spread.append(grad)
        total = total + part
    send_hidden(out_ref, 0, grad_spread)
    send_total(out_ref, 64, total * inv_rms)
    send_hidden(out_ref, 72, mixed)


def hidden_backward_kernel(wire_ref, middle_ref, spread_ref, preact_ref, act_ref, inv_ref, out_ref, grads_ref):
    inv_rms = inv_ref[0:1, :]
    grad_mixed = take_hidden(wire_ref, 0)
    grad_spread, total = [], 0.0
    for c in range(4):
        preact = preact_ref[c]
        _, slope = gelu_pair(preact)
        grad, part = hidden_backward(
            c, grad_mixed[c], act_ref[c], preact, slope, inv_rms, spread_ref[c], middle_ref, grads_ref
        )
        grad_spread.append(grad)
        total = total + part
    send_hidden(out_ref, 0, grad_spread)
    send_total(out_ref, 64, total * inv_rms)


def back_through(wire_ref, stream, grad, first_ref, gain_ref, first_grad_ref, gain_grad_ref, section_ref):
    grad_spread = take_features(wire_ref, 0)
    total = take_total(wire_ref, 64)
    gain = gain_column(gain_ref)
    scaled = (stream * gain).astype(BF16)
    norms = []
    for i in range(2):
        part = nt(scaled[i * 128 : i * 128 + 128], grad_spread[i]).astype(BF16)
        for h in range(2):
            first_grad_ref[h * 256 + i * 128 : h * 256 + i * 128 + 128, :] = part[:, h * 256 : h * 256 + 256]
        norms.append(nn(first_of(first_ref, i), grad_spread[i]))
    grad_norm = rows(norms)
    gain_part = jnp.sum(grad_norm * stream, axis=1, keepdims=True)
    gain_row = lanes([jnp.broadcast_to(gain_part[i * 128 : i * 128 + 128], (128, 128)).T[0:1] for i in range(2)])
    high = gain_row.astype(BF16).astype(F32)
    gain_grad_ref[...] = rows([high, gain_row - high, jnp.zeros((14, 256), F32)]).astype(BF16)
    result = grad.astype(F32) + grad_norm * gain - stream * (total / 8192.0)
    section_ref[...] = result.T.astype(BF16)
    return result.astype(BF16)


def fourth_grad(fourth_grad_ref, mixed, grad):
    for i in range(2):
        fourth_grad_ref[:, i * 128 : i * 128 + 128] = nt(mixed[i], grad[i * 128 : i * 128 + 128]).astype(BF16)


def features_turn_kernel(
    wire_ref, stream_ref, grad_ref, first_ref, gain_ref, last_fourth_ref, fourth_ref, mixed_ref,
    out_ref, next_ref, first_grad_ref, gain_grad_ref, section_grad_ref, fourth_grad_ref,
    section_ref, last_fourth_grad_ref,
):
    stream = stream_ref[...].astype(F32)
    grad = grad_ref[...]
    result = back_through(
        wire_ref, stream, grad, first_ref, gain_ref, first_grad_ref, gain_grad_ref, section_grad_ref
    )
    next_ref[...] = result
    send_grad(out_ref, 0, result, fourth_ref)
    fourth_grad(fourth_grad_ref, [mixed_ref[0], mixed_ref[1]], result)
    mixed = take_features(wire_ref, 72)
    section_ref[...] = leave_layer(stream, mixed, last_fourth_ref).astype(F32).T.astype(BF16)
    fourth_grad(last_fourth_grad_ref, mixed, grad)


def features_backward_kernel(
    wire_ref, stream_ref, grad_ref, first_ref, gain_ref, fourth_ref, mixed_ref,
    out_ref, next_ref, first_grad_ref, gain_grad_ref, section_grad_ref, fourth_grad_ref,
):
    result = back_through(
        wire_ref, stream_ref[...].astype(F32), grad_ref[...], first_ref, gain_ref,
        first_grad_ref, gain_grad_ref, section_grad_ref,
    )
    next_ref[...] = result
    send_grad(out_ref, 0, result, fourth_ref)
    fourth_grad(fourth_grad_ref, [mixed_ref[0], mixed_ref[1]], result)


def features_end_kernel(
    wire_ref, stream_ref, grad_ref, first_ref, gain_ref, first_grad_ref, gain_grad_ref, section_grad_ref
):
    back_through(
        wire_ref, stream_ref[...].astype(F32), grad_ref[...], first_ref, gain_ref,
        first_grad_ref, gain_grad_ref, section_grad_ref,
    )


def final_kernel(got_ref, second_ref, third_ref, first_ref, fourth_ref, gain_ref, out_ref, grad_ref):
    def total(start, size):
        return sum(got_ref[q, start : start + size, :].astype(F32) for q in range(4))

    for c in range(4):
        second_ref[0, c] = total(c * 256, 256)
        third_ref[0, c] = total(1024 + c * 256, 256)
    for i in range(2):
        for h in range(2):
            first_ref[0, i, :, h * 256 : h * 256 + 256] = total(ROWS_MID + h * 256 + i * 128, 128)
    both = total(ROWS_MID + ROWS_OUT, ROWS_OUT)
    fourth_ref[0, 0], fourth_ref[0, 1] = both[:, :128], both[:, 128:]
    start = ROWS_MID + 2 * ROWS_OUT
    for q in range(4):
        out_ref[0, 2 * q : 2 * q + 2] = got_ref[q, start : start + 256, :].reshape(2, 128, 256)
        grad_ref[0, 2 * q : 2 * q + 2] = got_ref[q, start + 256 : start + 512, :].reshape(2, 128, 256)
    gain = total(start + 512, 16)
    gain_ref[...] = gain[0:1] + gain[1:2]


def whole(shape):
    return pl.BlockSpec(shape, lambda *_: (0,) * len(shape))


def layer_block(size, layer, index):
    return pl.BlockSpec((1, size, 256), lambda *_: (layer, index, 0))


def middle_block(layer):
    return layer_block(ROWS_MID, layer, 0)


def first_block(layer):
    return layer_block(ROWS_OUT, layer, 4)


def fourth_block(layer):
    return layer_block(ROWS_OUT, layer, 5)


def gain_block(layer):
    return layer_block(16, layer, 192)


PARAMS = pltpu.CompilerParams(vmem_limit_bytes=56 * 1024 * 1024)


def run(kernel, name, specs, outs, *args, scalars=0):
    return pl.pallas_call(
        kernel,
        name=name,
        out_shape=[jax.ShapeDtypeStruct(shape, dtype) for shape, dtype in outs],
        grid_spec=pltpu.PrefetchScalarGridSpec(
            num_scalar_prefetch=scalars,
            grid=(1,),
            in_specs=specs,
            out_specs=[whole(shape) for shape, _ in outs],
        ),
        compiler_params=PARAMS,
    )(*args)


def swap(values, axis):
    return lax.all_to_all(values, axis, 0, 0, tiled=True)


SQUARE = ((256, 256), BF16)
MIXED = ((2, 512, 256), BF16)
HIDDEN = ((4, 256, 256), BF16)


def wire(size):
    return ((32, size, 128), BF16)


def body(inputs, cotangent, norm_gain, first_factor, second_factor, third_factor, fourth_factor):
    slot = lax.axis_index("pipe").astype(jnp.int32).reshape(1)
    tokens = pl.BlockSpec((2, 128, 256), lambda step, slot_ref: (slot_ref[0], 0, 0))
    square = whole((256, 256))
    mixed_spec = whole((2, 512, 256))
    hidden = whole((4, 256, 256))

    def wire_spec(size):
        return whole((32, size, 128))

    own = [first_factor, second_factor, third_factor, fourth_factor, norm_gain]
    (packed,) = run(
        pack_kernel, "pack", [whole(a.shape) for a in own], [((4, 3088, 256), BF16)], *own
    )
    weights = swap(packed, "pipe")

    sent, stream = run(
        start_kernel, "start", [tokens, first_block(0), gain_block(0)], [wire(72), SQUARE],
        slot, inputs, weights, weights, scalars=1,
    )
    streams, mixes, saved, sections = [stream], [], [], []
    for layer in range(3):
        got = swap(sent, "tensor")
        sent, *record = run(
            hidden_forward_kernel, "hidden_forward", [wire_spec(72), middle_block(layer)],
            [wire(64), HIDDEN, ((4, 256, 256), F32), HIDDEN, ((8, 256), F32)], got, weights,
        )
        saved.append(record)
        got = swap(sent, "tensor")
        specs = [wire_spec(64), square, fourth_block(layer), first_block(layer + 1), gain_block(layer + 1)]
        args = [got, streams[layer], weights, weights, weights]
        if layer < 2:
            sent, stream, mixed, section = run(
                between_kernel, "between", specs, [wire(72), SQUARE, MIXED, SQUARE], *args
            )
        else:
            sent, stream, mixed, section, grad = run(
                turn_kernel, "turn", specs + [tokens, fourth_block(3)],
                [wire(136), SQUARE, MIXED, SQUARE, SQUARE], slot, *args, cotangent, weights, scalars=1,
            )
        streams.append(stream)
        mixes.append(mixed)
        sections.append(section)
    got = swap(sent, "tensor")
    middle_grads, first_grads, fourth_grads, gain_grads, section_grads = ([None] * 4 for _ in range(5))
    sent, middle_grads[3] = run(
        hidden_turn_kernel, "hidden_turn", [wire_spec(136), middle_block(3)],
        [wire(136), ((2048, 256), BF16)], got, weights,
    )
    rest = [((512, 256), BF16), ((16, 256), BF16), SQUARE]
    for layer in (3, 2, 1, 0):
        got = swap(sent, "tensor")
        size = 136 if layer == 3 else 72
        specs = [wire_spec(size), square, square, first_block(layer), gain_block(layer)]
        args = [got, streams[layer], grad, weights, weights]
        if layer == 3:
            (sent, grad, first_grads[3], gain_grads[3], section_grads[3], fourth_grads[2], section,
             fourth_grads[3]) = run(
                features_turn_kernel, "features_turn", specs + [fourth_block(3), fourth_block(2), mixed_spec],
                [wire(64), SQUARE] + rest + [((512, 256), BF16), SQUARE, ((512, 256), BF16)],
                *args, weights, weights, mixes[2],
            )
            sections.append(section)
        elif layer > 0:
            (sent, grad, first_grads[layer], gain_grads[layer], section_grads[layer],
             fourth_grads[layer - 1]) = run(
                features_backward_kernel, "features_backward", specs + [fourth_block(layer - 1), mixed_spec],
                [wire(64), SQUARE] + rest + [((512, 256), BF16)], *args, weights, mixes[layer - 1],
            )
        else:
            first_grads[0], gain_grads[0], section_grads[0] = run(
                features_end_kernel, "features_end", specs, rest, *args
            )
        if layer > 0:
            got = swap(sent, "tensor")
            sent, middle_grads[layer - 1] = run(
                hidden_backward_kernel, "hidden_backward",
                [wire_spec(64), middle_block(layer - 1), hidden, hidden, hidden, whole((8, 256))],
                [wire(72), ((2048, 256), BF16)], got, weights, *saved[layer - 1],
            )
    parts = [middle_grads, first_grads, fourth_grads, sections, section_grads, gain_grads]
    whole_sent = jnp.stack([jnp.concatenate([part[layer] for part in parts]) for layer in range(4)])
    got = swap(whole_sent, "pipe")
    outs = [
        (second_factor.shape, F32), (third_factor.shape, F32), (first_factor.shape, F32),
        (fourth_factor.shape, F32), (norm_gain.shape, F32),
        ((1,) + inputs.shape, BF16), ((1,) + inputs.shape, BF16),
    ]
    second, third, first, fourth, gain, section_out, section_grad = run(
        final_kernel, "final", [whole(got.shape)], outs, got
    )
    return section_out, section_grad, gain, first, second, third, fourth


def solution(mesh):
    placed = (
        P(None, None, "tensor"),
        P(None, None, "tensor"),
        P("pipe", "tensor"),
        P("pipe", "tensor", None, None),
        P("pipe", "tensor", None, None),
        P("pipe", "tensor", None, None),
        P("pipe", "tensor", None, None),
    )
    return jax.shard_map(
        body,
        mesh=mesh,
        in_specs=placed,
        out_specs=(
            P("pipe", None, None, "tensor"),
            P("pipe", None, None, "tensor"),
            P("pipe", "tensor"),
            P("pipe", "tensor", None, None),
            P("pipe", "tensor", None, None),
            P("pipe", "tensor", None, None),
            P("pipe", "tensor", None, None),
        ),
        check_vma=False,
    )
```

time: 2460 us -> 490 us (0.20)
  blocking collectives: 1420 us -> 253 us
  local copies, waits for them, and re-layouts: 256 us -> 18.6 us
  starting transfers between devices: 258 us -> 25.6 us
  matrix products: 175 us -> 0 us
  waiting for transfers between devices: 235 us -> 118 us
  other arithmetic: 93.8 us -> 3.51 us
  Pallas kernels: 0 us -> 66.9 us
    psum x22 -> x0, blocking collectives: 1420 us -> none  [row_total(): return lax.psum(values, 'tensor')]
    all_to_all x0 -> x10, blocking collectives: none -> 253 us  [swap(): return lax.all_to_all(values, axis, 0, 0, tiled=True)]
    all_to_all x44 -> x6, starting transfers between devices: 208 us -> 25.6 us  [swap(): return lax.all_to_all(values, axis, 0, 0, tiled=True)]
    dot_general x121 -> x0, matrix products: 154 us -> none  [the longest x11 26.2 us: body(): jnp.einsum('tiac,tce->ciae', hidden_in, grad_pre, preferred_element_type=...]
    dynamic_slice x70 -> x0, local copies, waits for them, and re-layouts: 92.4 us -> none  [the longest x47 73.1 us: store_at(): former = lax.dynamic_index_in_dim(stored, micro_slot, 0, keepdims=False)]
    all_to_all x44 -> x6, waiting for transfers between devices: 202 us -> 118 us  [swap(): return lax.all_to_all(values, axis, 0, 0, tiled=True)]
    dynamic_update_slice x63 -> x0, other arithmetic: 76.8 us -> none  [store_at(): lax.dynamic_update_index_in_dim(stored, jnp.where(is_valid, member, forme...]
    pallas_call x0 -> x17, Pallas kernels: none -> 66.9 us  [run(): pl.pallas_call(kernel, name=name, out_shape=[jax.ShapeDtypeStruct(shape,...]
  transfers between devices with their start and end apart: 64 -> 6, of which waited for: 52 -> 6; matrix products, arithmetic and copies ran while one was open for 10% -> 2% of each run, Pallas kernels for 0% -> 0%
where the time goes in v1:
time: 490 us; the launch traced here: 486 us
  blocking collectives  253 us (52%)
  waiting for transfers between devices  118 us (24%)
  Pallas kernels  66.9 us (14%)
  starting transfers between devices  25.6 us (5%)
  local copies, waits for them, and re-layouts  18.6 us (4%)
    all_to_all x10, blocking collectives, swap(): return lax.all_to_all(values, axis, 0, 0, tiled=True)  253 us
    all_to_all x6, waiting for transfers between devices, swap(): return lax.all_to_all(values, axis, 0, 0, tiled=True)  118 us
    pallas_call x17, Pallas kernels, run(): pl.pallas_call(kernel, name=name, out_shape=[jax.ShapeDtypeStruct(shape,...  66.9 us
    all_to_all x6, starting transfers between devices, swap(): return lax.all_to_all(values, axis, 0, 0, tiled=True)  25.6 us
    unnamed x70, local copies, waits for them, and re-layouts  16.7 us
  transfers between devices with their start and end apart: 6, of which 6 were waited for; matrix products, arithmetic and copies ran while one was open for 2% of the time, Pallas kernels for 0%

profile of v1, /device:TPU:24, one launch (start us, length us, event | category | flops | bytes accessed | tf_op | source)
XLA Modules:
  0.0 485.9 jit_solution(1023722459131869652)
XLA Ops:
  0.6 4.5 pack.1
  5.2 5.3 %all-to-all-start = ((bf16[4,3088,256]{2,1,0:T(8,128)(2,1)}), bf16[4,3088,256]{2,1,0:T(8,128)(2,1)}, u32[]{:S(2)}, u32[]{:S(2)}) async-start(bf16[4,3088,256]{2,1,0:T(8,128)(2,1)} %pack.1), calls=%async_computation | async-start | bytes 12648448 | tf_op jit(solution)/shard_map/all_to_all | solution.py:426
  10.5 69.9 %all-to-all-done.first_ref.gain_ref.middle_ref.fourth_ref.last_fourth_ref = bf16[4,3088,256]{2,1,0:T(8,128)(2,1)} async-done(((bf16[4,3088,256]{2,1,0:T(8,128)(2,1)}), bf16[4,3088,256]{2,1,0:T(8,128)(2,1)}, u32[]{:S(2)}, u32[]{:S(2)}) %all-to-all-start) | async-done | bytes 6324256 | tf_op jit(solution)/shard_map/all_to_all | solution.py:426
  82.8 20.8 %all_to_all.80.wire_ref = bf16[32,72,128]{2,1,0:T(8,128)(2,1)} all-to-all(bf16[32,72,128]{2,1,0:T(8,128)(2,1)} %get-tuple-element.75), channel_id=1, replica_groups=mesh['pipe'=4,'tensor'=32] {'tensor'}, dimensions={0} | all-to-all | bytes 1179648 | tf_op jit(solution)/shard_map/all_to_all | solution.py:426
  107.1 16.2 %all_to_all.81.wire_ref = bf16[32,64,128]{2,1,0:T(8,128)(2,1)} all-to-all(bf16[32,64,128]{2,1,0:T(8,128)(2,1)} %get-tuple-element.76), channel_id=1, replica_groups=mesh['pipe'=4,'tensor'=32] {'tensor'}, dimensions={0} | all-to-all | bytes 1048576 | tf_op jit(solution)/shard_map/all_to_all | solution.py:426
  126.3 16.9 %all_to_all.82.wire_ref = bf16[32,72,128]{2,1,0:T(8,128)(2,1)} all-to-all(bf16[32,72,128]{2,1,0:T(8,128)(2,1)} %get-tuple-element.78), channel_id=1, replica_groups=mesh['pipe'=4,'tensor'=32] {'tensor'}, dimensions={0} | all-to-all | bytes 1179648 | tf_op jit(solution)/shard_map/all_to_all | solution.py:426
  146.7 16.2 %all_to_all.83.wire_ref = bf16[32,64,128]{2,1,0:T(8,128)(2,1)} all-to-all(bf16[32,64,128]{2,1,0:T(8,128)(2,1)} %get-tuple-element.79), channel_id=1, replica_groups=mesh['pipe'=4,'tensor'=32] {'tensor'}, dimensions={0} | all-to-all | bytes 1048576 | tf_op jit(solution)/shard_map/all_to_all | solution.py:426
  165.9 16.9 %all_to_all.84.wire_ref = bf16[32,72,128]{2,1,0:T(8,128)(2,1)} all-to-all(bf16[32,72,128]{2,1,0:T(8,128)(2,1)} %get-tuple-element.81), channel_id=1, replica_groups=mesh['pipe'=4,'tensor'=32] {'tensor'}, dimensions={0} | all-to-all | bytes 1179648 | tf_op jit(solution)/shard_map/all_to_all | solution.py:426
  186.3 16.2 %all_to_all.85.wire_ref = bf16[32,64,128]{2,1,0:T(8,128)(2,1)} all-to-all(bf16[32,64,128]{2,1,0:T(8,128)(2,1)} %get-tuple-element.82), channel_id=1, replica_groups=mesh['pipe'=4,'tensor'=32] {'tensor'}, dimensions={0} | all-to-all | bytes 1048576 | tf_op jit(solution)/shard_map/all_to_all | solution.py:426
  202.5 3.8 turn.1
  206.2 23.1 %all_to_all.86.wire_ref = bf16[32,136,128]{2,1,0:T(8,128)(2,1)} all-to-all(bf16[32,136,128]{2,1,0:T(8,128)(2,1)} %get-tuple-element.84), channel_id=1, replica_groups=mesh['pipe'=4,'tensor'=32] {'tensor'}, dimensions={0} | all-to-all | bytes 2228224 | tf_op jit(solution)/shard_map/all_to_all | solution.py:426
  229.4 5.6 %hidden_turn.1 = (bf16[32,136,128]{2,1,0:T(8,128)(2,1)}, bf16[2048,256]{1,0:T(8,128)(2,1)}) custom-call(bf16[32,136,128]{2,1,0:T(8,128)(2,1)} %all_to_all.86.wire_ref, bf16[4,3088,256]{2,1,0:T(8,128)(2,1)} %all-to-all-done.first_ref.gain_ref.middle_ref.fourth_ref.last_fourth_ref), custom_call_target="tpu_custom_call" | custom-call | tf_op jit(solution)/shard_map/hidden_turn/pallas_call | solution.py:411
  235.0 23.1 %all_to_all.87.wire_ref = bf16[32,136,128]{2,1,0:T(8,128)(2,1)} all-to-all(bf16[32,136,128]{2,1,0:T(8,128)(2,1)} %get-tuple-element.85), channel_id=1, replica_groups=mesh['pipe'=4,'tensor'=32] {'tensor'}, dimensions={0} | all-to-all | bytes 2228224 | tf_op jit(solution)/shard_map/all_to_all | solution.py:426
  258.1 4.1 features_turn.1
  262.2 16.2 %all_to_all.88.wire_ref = bf16[32,64,128]{2,1,0:T(8,128)(2,1)} all-to-all(bf16[32,64,128]{2,1,0:T(8,128)(2,1)} %get-tuple-element.89), channel_id=1, replica_groups=mesh['pipe'=4,'tensor'=32] {'tensor'}, dimensions={0} | all-to-all | bytes 1048576 | tf_op jit(solution)/shard_map/all_to_all | solution.py:426
  278.4 4.9 %hidden_backward.3 = (bf16[32,72,128]{2,1,0:T(8,128)(2,1)}, bf16[2048,256]{1,0:T(8,128)(2,1)}) custom-call(bf16[32,64,128]{2,1,0:T(8,128)(2,1)} %all_to_all.88.wire_ref, bf16[4,3088,256]{2,1,0:T(8,128)(2,1)} %all-to-all-done.first_ref.gain_ref.middle_ref.fourth_ref.last_fourth_ref, bf16[4,256,256]{2,1,0:T(8,128)(2,1)} %get-tuple-element.90.spread_ref, ...), custom_call_target="tpu_custom_call" | custom-call | tf_op jit(solution)/shard_map/hidden_backward/pallas_call | solution.py:411
  283.3 4.0 all-to-all-start.10
  287.4 12.2 %all-to-all-done.10.wire_ref = bf16[32,72,128]{2,1,0:T(8,128)(2,1)S(1)} async-done(((bf16[32,72,128]{2,1,0:T(8,128)(2,1)}), bf16[32,72,128]{2,1,0:T(8,128)(2,1)S(1)}, u32[]{:S(2)}, u32[]{:S(2)}) %all-to-all-start.10) | async-done | bytes 589856 | tf_op jit(solution)/shard_map/all_to_all | solution.py:426
  300.5 3.5 features_backward.2
  304.1 4.0 all-to-all-start.11
  308.3 11.4 %all-to-all-done.11.wire_ref = bf16[32,64,128]{2,1,0:T(8,128)(2,1)S(1)} async-done(((bf16[32,64,128]{2,1,0:T(8,128)(2,1)}), bf16[32,64,128]{2,1,0:T(8,128)(2,1)S(1)}, u32[]{:S(2)}, u32[]{:S(2)}) %all-to-all-start.11) | async-done | bytes 524320 | tf_op jit(solution)/shard_map/all_to_all | solution.py:426
  320.5 4.9 %hidden_backward.4 = (bf16[32,72,128]{2,1,0:T(8,128)(2,1)}, bf16[2048,256]{1,0:T(8,128)(2,1)}) custom-call(bf16[32,64,128]{2,1,0:T(8,128)(2,1)} %copy-done.4, bf16[4,3088,256]{2,1,0:T(8,128)(2,1)} %all-to-all-done.first_ref.gain_ref.middle_ref.fourth_ref.last_fourth_ref, bf16[4,256,256]{2,1,0:T(8,128)(2,1)} %get-tuple-element.98.spread_ref, ...), custom_call_target="tpu_custom_call" | custom-call | tf_op jit(solution)/shard_map/hidden_backward/pallas_call | solution.py:411
  325.4 4.2 all-to-all-start.12
  333.5 8.2 %all-to-all-done.12.wire_ref = bf16[32,72,128]{2,1,0:T(8,128)(2,1)S(1)} async-done(((bf16[32,72,128]{2,1,0:T(8,128)(2,1)}), bf16[32,72,128]{2,1,0:T(8,128)(2,1)S(1)}, u32[]{:S(2)}, u32[]{:S(2)}) %all-to-all-start.12) | async-done | bytes 589856 | tf_op jit(solution)/shard_map/all_to_all | solution.py:426
  342.6 3.6 features_backward.3
  346.1 3.9 all-to-all-start.13
  353.1 8.5 %all-to-all-done.13.wire_ref = bf16[32,64,128]{2,1,0:T(8,128)(2,1)S(1)} async-done(((bf16[32,64,128]{2,1,0:T(8,128)(2,1)}), bf16[32,64,128]{2,1,0:T(8,128)(2,1)S(1)}, u32[]{:S(2)}, u32[]{:S(2)}) %all-to-all-start.13) | async-done | bytes 524320 | tf_op jit(solution)/shard_map/all_to_all | solution.py:426
  362.4 4.9 %hidden_backward.5 = (bf16[32,72,128]{2,1,0:T(8,128)(2,1)}, bf16[2048,256]{1,0:T(8,128)(2,1)}) custom-call(bf16[32,64,128]{2,1,0:T(8,128)(2,1)} %copy-done.5, bf16[4,3088,256]{2,1,0:T(8,128)(2,1)} %all-to-all-done.first_ref.gain_ref.middle_ref.fourth_ref.last_fourth_ref, bf16[4,256,256]{2,1,0:T(8,128)(2,1)} %get-tuple-element.106.spread_ref, ...), custom_call_target="tpu_custom_call" | custom-call | tf_op jit(solution)/shard_map/hidden_backward/pallas_call | solution.py:411
  367.3 4.0 all-to-all-start.14
  376.1 7.5 %all-to-all-done.14.wire_ref = bf16[32,72,128]{2,1,0:T(8,128)(2,1)S(1)} async-done(((bf16[32,72,128]{2,1,0:T(8,128)(2,1)}), bf16[32,72,128]{2,1,0:T(8,128)(2,1)S(1)}, u32[]{:S(2)}, u32[]{:S(2)}) %all-to-all-start.14) | async-done | bytes 589856 | tf_op jit(solution)/shard_map/all_to_all | solution.py:426
  393.5 87.1 %all_to_all.89.got_ref = bf16[4,3600,256]{2,1,0:T(8,128)(2,1)} all-to-all(bf16[4,3600,256]{2,1,0:T(8,128)(2,1)S(1)} %pad_maximum_fusion), channel_id=1, replica_groups=mesh['pipe'=4,'tensor'=32] {'pipe'}, dimensions={0} | all-to-all | bytes 14745600 | tf_op jit(solution)/shard_map/all_to_all | solution.py:426
  480.6 5.3 %final.1 = (f32[1,4,256,256]{3,2,1,0:T(8,128)}, f32[1,4,256,256]{3,2,1,0:T(8,128)}, f32[1,2,128,512]{3,2,1,0:T(8,128)}, f32[1,2,512,128]{3,2,1,0:T(8,128)}, f32[...) custom-call(bf16[4,3600,256]{2,1,0:T(8,128)(2,1)} %all_to_all.89.got_ref), custom_call_target="tpu_custom_call" | custom-call | tf_op jit(solution)/shard_map/final/pallas_call | solution.py:411
  (82 shorter events, 44.0 us)
Async XLA Ops:
  5.2 75.2 %all-to-all-start = ((bf16[4,3088,256]{2,1,0:T(8,128)(2,1)}), bf16[4,3088,256]{2,1,0:T(8,128)(2,1)}, u32[]{:S(2)}, u32[]{:S(2)}) async-start(bf16[4,3088,256]{2,1,0:T(8,128)(2,1)} %pack.1), calls=%async_computation | async-start | bytes 12648448 | tf_op jit(solution)/shard_map/all_to_all | solution.py:426
  283.3 4.0 copy-start.8
  283.3 16.3 %all-to-all-start.10 = ((bf16[32,72,128]{2,1,0:T(8,128)(2,1)}), bf16[32,72,128]{2,1,0:T(8,128)(2,1)S(1)}, u32[]{:S(2)}, u32[]{:S(2)}) async-start(bf16[32,72,128]{2,1,0:T(8,128)(2,1)} %get-tuple-element.94), calls=%async_computation.10 | async-start | bytes 1179648 | tf_op jit(solution)/shard_map/all_to_all | solution.py:426
  299.6 0.9 copy-start.3
  300.5 7.6 %copy-start.15 = (bf16[512,256]{1,0:T(8,128)(2,1)S(1)}, bf16[512,256]{1,0:T(8,128)(2,1)}, u32[]{:S(2)}) copy-start(bf16[512,256]{1,0:T(8,128)(2,1)} %get-tuple-element.131) | copy-start | bytes 786436
  300.5 7.6 %copy-start.13 = (bf16[512,256]{1,0:T(8,128)(2,1)S(1)}, bf16[512,256]{1,0:T(8,128)(2,1)}, u32[]{:S(2)}) copy-start(bf16[512,256]{1,0:T(8,128)(2,1)} %get-tuple-element.132) | copy-start | bytes 786436
  304.1 4.1 copy-start.21
  304.1 4.2 copy-start.20
  304.1 4.2 copy-start.23
  304.1 15.6 %all-to-all-start.11 = ((bf16[32,64,128]{2,1,0:T(8,128)(2,1)}), bf16[32,64,128]{2,1,0:T(8,128)(2,1)S(1)}, u32[]{:S(2)}, u32[]{:S(2)}) async-start(bf16[32,64,128]{2,1,0:T(8,128)(2,1)} %get-tuple-element.97), calls=%async_computation.11 | async-start | bytes 1048576 | tf_op jit(solution)/shard_map/all_to_all | solution.py:426
  319.7 0.8 copy-start.4
  325.4 4.3 copy-start.6
  325.4 16.4 %all-to-all-start.12 = ((bf16[32,72,128]{2,1,0:T(8,128)(2,1)}), bf16[32,72,128]{2,1,0:T(8,128)(2,1)S(1)}, u32[]{:S(2)}, u32[]{:S(2)}) async-start(bf16[32,72,128]{2,1,0:T(8,128)(2,1)} %get-tuple-element.102), calls=%async_computation.12 | async-start | bytes 1179648 | tf_op jit(solution)/shard_map/all_to_all | solution.py:426
  329.6 1.1 copy-start.14
  329.7 1.8 copy-start.11
  329.7 2.5 copy-start.18
  329.7 3.2 copy-start.19
  341.7 0.8 copy-start.1
  342.6 7.5 %copy-start.22 = (bf16[16,256]{1,0:T(8,128)(2,1)S(1)}, bf16[16,256]{1,0:T(8,128)(2,1)}, u32[]{:S(2)}) copy-start(bf16[16,256]{1,0:T(8,128)(2,1)} %get-tuple-element.129) | copy-start | bytes 24580
  342.6 8.1 %copy-start.7 = (bf16[2048,256]{1,0:T(8,128)(2,1)S(1)}, bf16[2048,256]{1,0:T(8,128)(2,1)}, u32[]{:S(2)}) copy-start(bf16[2048,256]{1,0:T(8,128)(2,1)} %get-tuple-element.118) | copy-start | bytes 3145732
  346.1 15.5 %all-to-all-start.13 = ((bf16[32,64,128]{2,1,0:T(8,128)(2,1)}), bf16[32,64,128]{2,1,0:T(8,128)(2,1)S(1)}, u32[]{:S(2)}, u32[]{:S(2)}) async-start(bf16[32,64,128]{2,1,0:T(8,128)(2,1)} %get-tuple-element.105), calls=%async_computation.13 | async-start | bytes 1048576 | tf_op jit(solution)/shard_map/all_to_all | solution.py:426
  350.0 1.7 copy-start.16
  350.0 2.4 copy-start.10
  361.6 0.8 copy-start.5
  362.4 12.1 %copy-start.24 = (bf16[16,256]{1,0:T(8,128)(2,1)S(1)}, bf16[16,256]{1,0:T(8,128)(2,1)}, u32[]{:S(2)}) copy-start(bf16[16,256]{1,0:T(8,128)(2,1)} %get-tuple-element.123) | copy-start | bytes 24580
  367.3 7.8 %copy-start.9 = (bf16[2048,256]{1,0:T(8,128)(2,1)S(1)}, bf16[2048,256]{1,0:T(8,128)(2,1)}, u32[]{:S(2)}) copy-start(bf16[2048,256]{1,0:T(8,128)(2,1)} %get-tuple-element.110) | copy-start | bytes 3145732
  367.3 16.3 %all-to-all-start.14 = ((bf16[32,72,128]{2,1,0:T(8,128)(2,1)}), bf16[32,72,128]{2,1,0:T(8,128)(2,1)S(1)}, u32[]{:S(2)}, u32[]{:S(2)}) async-start(bf16[32,72,128]{2,1,0:T(8,128)(2,1)} %get-tuple-element.111), calls=%async_computation.14 | async-start | bytes 1179648 | tf_op jit(solution)/shard_map/all_to_all | solution.py:426
  383.6 0.8 copy-start.2
  384.4 2.9 copy-start
  384.4 3.8 copy-start.12
  384.4 3.9 copy-start.17
